TPU v7x, 256 devices: a whole 4x4x8 slice. The times are simulated.
256 devices in a mesh: rows: 64 (over z_lo, y, x, core), cols: 4 (over z_hi).
Axes of the slice: x: 4, y: 4, z: 8 (z_hi: 4, z_lo: 2; z = z_hi * 2 + z_lo), core: 2. Of those that a mesh axis runs over, the one named last changes fastest.
Arguments:
- design: bfloat16 [256, 1048576], P(None, 'rows'), may hold values from -0.28125 to 0.28125
- targets: bfloat16 [128, 1048576], P('cols', 'rows'), may hold values from -8 to 8
- flip_bits: int32 [2, 1048576], P(None, 'rows'), may hold values from 0 to 1
- listed: int32 [2, 32768], P(None, 'rows'), may hold values from 0 to 16383
- block_order: int32 [2, 64, 16], P(None, 'rows'), may hold values from 0 to 15, each once within a row
Outputs:
- solution: float32 [256, 128], P(None, 'cols')
- residual: float32 [128, 1048576], P('cols', 'rows')
Inputs may be any that keep to these rules, and one draw needn't show every extreme that they name: A group's listed rows are its own rows, counted from its first row; repeats may occur. `block_order`: for each step and group the 16 entries are a permutation.
All inputs are finite; a program needn't handle non-finite values.
Results may differ from a plain program's by a relative error of at most 0.017.
Values sent between devices are 32-bit elements; how exact they have to be, the bound alone decides.
A program may use at most 64 MiB of HBM per device.

v0:
```python
import math
import jax
import jax.numpy as jnp
from jax import lax
from jax.sharding import PartitionSpec as P


def on_device(design, targets, flip_bits, listed, block_order):
    unknowns, rows_here = design.shape
    steps_count = flip_bits.shape[0]
    blocks_count = block_order.shape[2]
    block_len = rows_here // blocks_count
    pick_count = listed.shape[1]
    col_share = unknowns // lax.axis_size("cols")
    inv_root = 1.0 / math.sqrt(block_len)
    keep_scale = math.sqrt(rows_here / pick_count)
    own_rows = lax.dynamic_slice_in_dim(design, lax.axis_index("cols") * col_share, col_share, 0)
    positions = jnp.arange(block_len, dtype=jnp.int32)[:, None]
    block_ids = jnp.arange(blocks_count, dtype=jnp.int32)[:, None]
    unit_eye = jnp.eye(unknowns, dtype=jnp.float32)

    def misfit_of(solution):
        product = lax.dot_general(
            solution.astype(jnp.bfloat16),
            design,
            (((0,), (0,)), ((), ())),
            preferred_element_type=jnp.float32,
        )
        return product - targets.astype(jnp.float32)

    solution = jnp.zeros((unknowns, targets.shape[0]), jnp.float32)
    for step_index in range(steps_count):
        sign_rows = (
            (2 * flip_bits[step_index] - 1).astype(jnp.bfloat16).reshape(blocks_count, block_len)
        )
        chosen = listed[step_index]
        order_now = block_order[step_index, 0]
        target_block = chosen // block_len
        within = chosen % block_len
        source = jnp.sum(
            jnp.where(target_block[None, :] == block_ids, order_now[:, None], 0), axis=0
        )
        parity = jnp.zeros((block_len, pick_count), jnp.int32)
        for bit_index in range(block_len.bit_length() - 1):
            parity = parity ^ positions >> bit_index & 1 & (within[None, :] >> bit_index & 1)
        walsh = (1 - 2 * parity).astype(jnp.bfloat16)
        placed = (source[None, :] == block_ids).astype(jnp.bfloat16)
        table = (placed[:, None, :] * sign_rows[:, :, None] * walsh[None, :, :]).reshape(
            rows_here, pick_count
        )
        mixed_rows = (
            jnp.dot(own_rows, table, preferred_element_type=jnp.float32) * inv_root
        ).astype(jnp.bfloat16)
        summed = lax.psum((mixed_rows.astype(jnp.float32) * keep_scale)[None], "rows")
        whole_sketch = lax.all_gather(summed, "cols", axis=1, tiled=True)
        gram_stack = jnp.einsum(
            "npm,nqm->npq", whole_sketch, whole_sketch, precision=lax.Precision.HIGHEST
        )
        shift = jnp.trace(gram_stack, axis1=1, axis2=2) / unknowns
        gram_now = (gram_stack + shift[:, None, None] * unit_eye[None])[0]
        if step_index == 0:
            misfit_half = -targets
        else:
            misfit_half = misfit_of(solution).astype(jnp.bfloat16)
        local_grad = lax.dot_general(
            design, misfit_half, (((1,), (1,)), ((), ())), preferred_element_type=jnp.float32
        )
        gradient = lax.psum(local_grad, "rows")
        factor = jnp.linalg.cholesky(gram_now)
        solution = solution - jax.scipy.linalg.cho_solve((factor, True), gradient)
    return (solution, misfit_of(solution))


def solution(mesh):
    return jax.shard_map(
        on_device,
        mesh=mesh,
        in_specs=(
            P(None, "rows"),
            P("cols", "rows"),
            P(None, "rows"),
            P(None, "rows"),
            P(None, "rows", None),
        ),
        out_specs=(P(None, "cols"), P("cols", "rows")),
        check_vma=False,
    )
```

profile of v0, /device:TPU:32, one launch (start us, length us, event | category | flops | bytes accessed | tf_op | source)
XLA Modules:
  0.0 1007.5 jit_solution(7467058959739676185)
XLA Ops:
  7.2 0.0 all-reduce.4.cloned.1.call-start
  7.3 0.8 and_select_fusion.3
  8.1 0.7 slice_bitcast_fusion.13
  8.8 0.1 select_reduce_fusion.6
  8.9 1.4 convert_reduce_fusion.1
  10.4 2.0 subtract_convert_fusion.1
  12.4 2.8 bitcast_multiply_fusion.2
  15.2 3.7 fusion.32
  18.9 2.0 subtract_convert_fusion
  20.9 2.8 bitcast_multiply_fusion
  23.7 3.7 fusion.20
  27.4 0.0 all-reduce.4.cloned.1.call-update
  27.4 6.0 fusion.35
  33.4 279.1 %psum.29 = f32[256,32]{0,1:T(8,128)S(1)} all-reduce(f32[256,32]{0,1:T(8,128)S(1)} %fusion.35), channel_id=1, replica_groups=mesh['rows'=64,'cols'=4] {'rows'}, use_global_device_ids=true, to_apply=%region_7.9 | all-reduce | flops 8192 | bytes 65536 | tf_op jit(solution)/shard_map/psum | solution.py:68
  312.5 231.7 %all-reduce.4.cloned.1.call-done = (f32[1,64,512]{2,1,0:T(8,128)}, f32[1,64,512]{2,1,0:T(8,128)}) async-done(((f32[1,64,512]{2,1,0:T(8,128)}, f32[1,64,512]{2,1,0:T(8,128)}), (f32[1,64,512]{2,1,0:T(8,128)}, f32[1,64,512]{2,1,0:T(8,128)})) %all-reduce.4.cloned.1.call-update) | async-done | bytes 262160 | tf_op jit(solution)/shard_map/psum | solution.py:54
  544.2 18.6 %all_gather.6 = f32[1,256,512]{2,1,0:T(8,128)S(1)} all-gather(f32[1,64,512]{2,1,0:T(8,128)} %get-tuple-element.39), channel_id=1, replica_groups=mesh['rows'=64,'cols'=4] {'cols'}, dimensions={1}, use_global_device_ids=true | all-gather | bytes 655360 | tf_op jit(solution)/shard_map/all_gather | solution.py:55
  562.8 1.2 select_reduce_fusion.1
  564.7 0.1 copy.15
  564.9 11.7 %cholesky.130 = f32[128,128]{1,0:T(8,128)S(1)} custom-call(f32[128,128]{1,0:T(8,128)S(1)} %cholesky.194), custom_call_target="Cholesky" | custom-call | tf_op jit(solution)/shard_map/jit(cholesky)/cholesky | solution.py:69
  576.7 9.8 custom-call.15
  586.5 0.2 constant_dynamic-update-slice_fusion.3
  586.7 0.3 convolution_subtract_fusion.3
  587.0 11.7 %cholesky.147 = f32[128,128]{1,0:T(8,128)S(1)} custom-call(f32[128,128]{1,0:T(8,128)S(1)} %convolution_subtract_fusion.3), custom_call_target="Cholesky" | custom-call | tf_op jit(solution)/shard_map/jit(cholesky)/cholesky | solution.py:69
  598.7 0.6 compare_reduce_fusion.2
  599.3 0.6 compare_reduce_fusion.3
  601.2 0.1 triangular_solve.88
  601.3 4.0 while.4
  601.6 0.6 fusion.101
  602.1 1.3 bitcast_dynamic-update-slice_fusion.4
  603.5 0.6 fusion.101
  604.1 1.3 bitcast_dynamic-update-slice_fusion.4
  605.4 19.7 %custom-call.16 = f32[2,128,128]{1,2,0:T(8,128)S(1)} custom-call(f32[2,128,128]{2,1,0:T(8,128)S(1)} %get-tuple-element.18), custom_call_target="InvertDiagBlocksLowerTriangular" | custom-call | tf_op jit(solution)/shard_map/jit(_cho_solve)/triangular_solve | solution.py:70
  625.0 0.2 fusion.50
  625.2 0.2 convolution_subtract_fusion.7
  625.4 0.3 fusion.52
  625.7 0.2 fusion.51
  626.0 0.2 convolution_subtract_fusion.6
  626.2 0.2 fusion.49
  626.4 0.0 copy-start.2
  626.4 9.9 convolution_bitcast_fusion
  636.3 277.7 %psum.31 = f32[256,32]{0,1:T(8,128)S(1)} all-reduce(f32[256,32]{0,1:T(8,128)S(1)} %convolution_bitcast_fusion), channel_id=1, replica_groups=mesh['rows'=64,'cols'=4] {'rows'}, use_global_device_ids=true, to_apply=%region_11.14 | all-reduce | flops 8192 | bytes 65536 | tf_op jit(solution)/shard_map/psum | solution.py:68
  914.0 15.9 %all_gather.7 = f32[1,256,512]{2,1,0:T(8,128)S(1)} all-gather(f32[1,64,512]{2,1,0:T(8,128)S(1)} %copy-done.2), channel_id=1, replica_groups=mesh['rows'=64,'cols'=4] {'cols'}, dimensions={1}, use_global_device_ids=true | all-gather | bytes 655360 | tf_op jit(solution)/shard_map/all_gather | solution.py:55
  929.8 1.2 select_reduce_fusion
  931.7 0.1 copy.18
  931.9 11.7 %cholesky.164 = f32[128,128]{1,0:T(8,128)S(1)} custom-call(f32[128,128]{1,0:T(8,128)S(1)} %cholesky.197), custom_call_target="Cholesky" | custom-call | tf_op jit(solution)/shard_map/jit(cholesky)/cholesky | solution.py:69
  943.7 9.8 custom-call.17
  953.5 0.2 constant_dynamic-update-slice_fusion.1
  953.7 0.3 convolution_subtract_fusion.2
  954.0 11.7 %cholesky.181 = f32[128,128]{1,0:T(8,128)S(1)} custom-call(f32[128,128]{1,0:T(8,128)S(1)} %convolution_subtract_fusion.2), custom_call_target="Cholesky" | custom-call | tf_op jit(solution)/shard_map/jit(cholesky)/cholesky | solution.py:69
  965.7 0.7 compare_reduce_fusion
  966.5 0.6 compare_reduce_fusion.1
  968.5 4.4 while.5
  968.8 0.6 fusion.102
  969.4 1.4 bitcast_dynamic-update-slice_fusion.5
  970.8 0.6 fusion.102
  971.4 1.4 bitcast_dynamic-update-slice_fusion.5
  972.9 19.7 %custom-call.18 = f32[2,128,128]{1,2,0:T(8,128)S(1)} custom-call(f32[2,128,128]{2,1,0:T(8,128)S(1)} %get-tuple-element.19), custom_call_target="InvertDiagBlocksLowerTriangular" | custom-call | tf_op jit(solution)/shard_map/jit(_cho_solve)/triangular_solve | solution.py:70
  992.5 0.2 fusion.54
  992.7 0.2 convolution_subtract_fusion.5
  992.9 0.3 fusion.56
  993.2 0.2 fusion.55
  993.5 0.2 convolution_subtract_fusion.4
  993.7 0.2 fusion.53
  993.9 6.3 convolution_subtract_fusion
  (42 shorter events, 0.6 us)
Async XLA Ops:
  7.2 537.0 %all-reduce.4.cloned.1.call-start = ((), (), s32[]{:S(2)}) async-start(), calls=%async_computation | async-start | bytes 524288 | tf_op jit(solution)/shard_map/psum | solution.py:54
  10.3 4.9 slice-start
  12.4 2.8 slice-start.1
  23.7 3.7 copy-start
  626.4 287.6 %copy-start.2 = (f32[1,64,512]{2,1,0:T(8,128)S(1)}, f32[1,64,512]{2,1,0:T(8,128)}, u32[]{:S(2)}) copy-start(f32[1,64,512]{2,1,0:T(8,128)} %get-tuple-element.38) | copy-start | bytes 393220
  993.9 6.3 copy-start.1
Sparse Core Ops, SparseCore 0:
  27.5 516.6 all-reduce.3
where the time goes:
time: 1010 us
  blocking collectives  591 us (59%)
  waiting for transfers between devices  232 us (23%)
  other arithmetic  121 us (12%)
  matrix products  35.3 us (3%)
  between operations  18.9 us (2%)
    psum x2, blocking collectives, on_device(): gradient = lax.psum(local_grad, 'rows')  557 us
    psum x1, waiting for transfers between devices, on_device(): lax.psum((mixed_rows.astype(jnp.float32) * keep_scale)[None], 'rows')  232 us
    another operation x14, other arithmetic, on_device(): factor = jnp.linalg.cholesky(gram_now)  69.2 us
    another operation x5, other arithmetic, on_device(): solution = solution - jax.scipy.linalg.cho_solve((factor, True), gradient)  39.4 us
    all_gather x2, blocking collectives, on_device(): whole_sketch = lax.all_gather(summed, 'cols', axis=1, tiled=True)  34.5 us
  transfers between devices with their start and end apart: 1, of which 1 were waited for; matrix products, arithmetic and copies ran while one was open for 1% of the time, Pallas kernels for 0%

commit v1 on v0

--- a/solution.py
+++ b/solution.py
@@ -3,6 +3,7 @@
 import jax.numpy as jnp
 from jax import lax
 from jax.sharding import PartitionSpec as P
+from jax.lax import all_gather
 
 
 def on_device(design, targets, flip_bits, listed, block_order):
@@ -65,7 +66,7 @@
         local_grad = lax.dot_general(
             design, misfit_half, (((1,), (1,)), ((), ())), preferred_element_type=jnp.float32
         )
-        gradient = lax.psum(local_grad, "rows")
+        gradient = jnp.sum(all_gather(local_grad, "rows"), 0)
         factor = jnp.linalg.cholesky(gram_now)
         solution = solution - jax.scipy.linalg.cho_solve((factor, True), gradient)
     return (solution, misfit_of(solution))

time: 1010 us -> 799 us (0.79)
  blocking collectives: 591 us -> 37.6 us
  waiting for transfers between devices: 232 us -> 563 us
    psum x2 -> x0, blocking collectives: 557 us -> none  [on_device(): gradient = lax.psum(local_grad, 'rows')]
    psum x1, waiting for transfers between devices: 232 us -> 510 us  [on_device(): lax.psum((mixed_rows.astype(jnp.float32) * keep_scale)[None], 'rows')]
    all_gather x0 -> x2, waiting for transfers between devices: none -> 53 us  [on_device(): gradient = jnp.sum(all_gather(local_grad, 'rows'), 0)]
  transfers between devices with their start and end apart: 1 -> 3, of which waited for: 1 -> 3; matrix products, arithmetic and copies ran while one was open for 1% -> 16% of each run, Pallas kernels for 0% -> 0%
where the time goes in v1:
time: 799 us; the launch traced here: 791 us
  waiting for transfers between devices  563 us (70%)
  other arithmetic  121 us (15%)
  blocking collectives  37.6 us (5%)
  matrix products  36.2 us (5%)
  between operations  18.4 us (2%)
  local copies, waits for them, and re-layouts  13.5 us (2%)
    psum x1, waiting for transfers between devices, on_device(): lax.psum((mixed_rows.astype(jnp.float32) * keep_scale)[None], 'rows')  510 us
    another operation x14, other arithmetic, on_device(): factor = jnp.linalg.cholesky(gram_now)  69.2 us
    all_gather x2, waiting for transfers between devices, on_device(): gradient = jnp.sum(all_gather(local_grad, 'rows'), 0)  53 us
    another operation x5, other arithmetic, on_device(): solution = solution - jax.scipy.linalg.cho_solve((factor, True), gradient)  39.4 us
    all_gather x2, blocking collectives, on_device(): whole_sketch = lax.all_gather(summed, 'cols', axis=1, tiled=True)  37.6 us
    dot_general x2, matrix products, on_device(): lax.dot_general(design, misfit_half, (((1,), (1,)), ((), ())), preferred_...  17.1 us
  transfers between devices with their start and end apart: 3, of which 3 were waited for; matrix products, arithmetic and copies ran while one was open for 16% of the time, Pallas kernels for 0%

profile of v1, /device:TPU:32, one launch (start us, length us, event | category | flops | bytes accessed | tf_op | source)
XLA Modules:
  0.0 790.6 jit_solution(14491040255093824703)
XLA Ops:
  7.3 0.8 and_select_fusion.3
  8.1 0.7 slice_bitcast_fusion.13
  8.8 0.1 select_reduce_fusion.6
  8.9 1.4 convert_reduce_fusion.1
  10.4 2.0 subtract_convert_fusion.1
  12.4 2.8 bitcast_multiply_fusion.2
  15.2 3.7 fusion.32
  18.9 2.0 subtract_convert_fusion
  20.9 2.8 bitcast_multiply_fusion
  23.7 3.7 fusion.20
  27.4 6.6 fusion.35
  34.1 510.1 %all-reduce.4.cloned.1.call-done = (f32[1,64,512]{2,1,0:T(8,128)}, f32[1,64,512]{2,1,0:T(8,128)}) async-done(((f32[1,64,512]{2,1,0:T(8,128)}, f32[1,64,512]{2,1,0:T(8,128)}), (f32[1,64,512]{2,1,0:T(8,128)}, f32[1,64,512]{2,1,0:T(8,128)})) %all-reduce.4.cloned.1.call-update) | async-done | bytes 262160 | tf_op jit(solution)/shard_map/psum | solution.py:55
  544.2 19.0 %all_gather.18 = f32[1,256,512]{2,1,0:T(8,128)S(1)} all-gather(f32[1,64,512]{2,1,0:T(8,128)} %get-tuple-element.39), channel_id=1, replica_groups=mesh['rows'=64,'cols'=4] {'cols'}, dimensions={1}, use_global_device_ids=true | all-gather | bytes 655360 | tf_op jit(solution)/shard_map/all_gather | solution.py:56
  563.1 1.2 select_reduce_fusion.1
  565.0 0.1 copy.21
  565.2 11.7 %cholesky.130 = f32[128,128]{1,0:T(8,128)S(1)} custom-call(f32[128,128]{1,0:T(8,128)S(1)} %cholesky.194), custom_call_target="Cholesky" | custom-call | tf_op jit(solution)/shard_map/jit(cholesky)/cholesky | solution.py:70
  577.0 9.8 %custom-call.15 = f32[1,128,128]{1,2,0:T(8,128)S(1)} custom-call(f32[1,128,128]{2,1,0:T(8,128)S(1)} %get-tuple-element.55), custom_call_target="InvertDiagBlocksLowerTriangular" | custom-call | tf_op jit(solution)/shard_map/jit(cholesky)/cholesky | solution.py:70
  586.8 0.2 constant_dynamic-update-slice_fusion.3
  587.0 0.3 convolution_subtract_fusion.3
  587.3 11.7 %cholesky.147 = f32[128,128]{1,0:T(8,128)S(1)} custom-call(f32[128,128]{1,0:T(8,128)S(1)} %convolution_subtract_fusion.3), custom_call_target="Cholesky" | custom-call | tf_op jit(solution)/shard_map/jit(cholesky)/cholesky | solution.py:70
  599.0 0.7 compare_reduce_fusion.2
  599.8 0.6 compare_reduce_fusion.3
  601.8 4.2 while.4
  602.0 0.6 fusion.101
  602.6 1.4 bitcast_dynamic-update-slice_fusion.4
  604.1 0.6 fusion.101
  604.7 1.4 bitcast_dynamic-update-slice_fusion.4
  606.1 19.7 %custom-call.16 = f32[2,128,128]{1,2,0:T(8,128)S(1)} custom-call(f32[2,128,128]{2,1,0:T(8,128)S(1)} %get-tuple-element.18), custom_call_target="InvertDiagBlocksLowerTriangular" | custom-call | tf_op jit(solution)/shard_map/jit(_cho_solve)/triangular_solve | solution.py:71
  625.8 28.6 %all-gather.5.cloned.1.call-done = f32[16384,32]{0,1:T(8,128)} async-done(((f32[256,32]{0,1:T(8,128)}), f32[16384,32]{0,1:T(8,128)}) %all-gather.5.cloned.1.call-update) | async-done | bytes 2097168 | tf_op jit(solution)/shard_map/all_gather | solution.py:69
  654.3 2.2 copy.27
  656.6 0.2 bitcast_reduce_fusion.1
  656.7 0.2 fusion.50
  656.9 0.2 convolution_subtract_fusion.7
  657.1 0.2 fusion.52
  657.3 0.2 fusion.51
  657.5 0.2 convolution_subtract_fusion.6
  657.7 0.2 fusion.49
  657.9 10.5 %convolution_bitcast_fusion = f32[256,32]{0,1:T(8,128)} fusion(bf16[256,16384]{1,0:T(8,128)(2,1)} %param.8, bf16[32,16384]{1,0:T(8,128)(2,1)S(1)} %copy-done, f32[128,32]{0,1:T(8,128)S(1)} %fusion.51, f32[128,32]{0,1:T(8,128)S(1)} %fusion.49), kind=kOutput, calls=%fused_computation.31 | convolution fusion | flops 538468352 | bytes 9502720 | tf_op jit(solution)/shard_map/dot_general | solution.py:66
  668.5 18.7 %all_gather.21 = f32[1,256,512]{2,1,0:T(8,128)S(1)} all-gather(f32[1,64,512]{2,1,0:T(8,128)S(1)} %copy-done.2), channel_id=1, replica_groups=mesh['rows'=64,'cols'=4] {'cols'}, dimensions={1}, use_global_device_ids=true | all-gather | bytes 655360 | tf_op jit(solution)/shard_map/all_gather | solution.py:56
  687.1 1.2 select_reduce_fusion
  689.0 0.1 copy.24
  689.2 11.7 %cholesky.164 = f32[128,128]{1,0:T(8,128)S(1)} custom-call(f32[128,128]{1,0:T(8,128)S(1)} %cholesky.197), custom_call_target="Cholesky" | custom-call | tf_op jit(solution)/shard_map/jit(cholesky)/cholesky | solution.py:70
  701.0 9.8 %custom-call.17 = f32[1,128,128]{1,2,0:T(8,128)S(1)} custom-call(f32[1,128,128]{2,1,0:T(8,128)S(1)} %get-tuple-element.59), custom_call_target="InvertDiagBlocksLowerTriangular" | custom-call | tf_op jit(solution)/shard_map/jit(cholesky)/cholesky | solution.py:70
  710.8 0.2 constant_dynamic-update-slice_fusion.1
  711.0 0.3 convolution_subtract_fusion.2
  711.3 11.7 %cholesky.181 = f32[128,128]{1,0:T(8,128)S(1)} custom-call(f32[128,128]{1,0:T(8,128)S(1)} %convolution_subtract_fusion.2), custom_call_target="Cholesky" | custom-call | tf_op jit(solution)/shard_map/jit(cholesky)/cholesky | solution.py:70
  723.1 0.6 compare_reduce_fusion
  723.7 0.6 compare_reduce_fusion.1
  725.7 4.2 while.5
  725.9 0.6 fusion.102
  726.5 1.4 bitcast_dynamic-update-slice_fusion.5
  727.9 0.6 fusion.102
  728.5 1.4 bitcast_dynamic-update-slice_fusion.5
  729.9 19.7 %custom-call.18 = f32[2,128,128]{1,2,0:T(8,128)S(1)} custom-call(f32[2,128,128]{2,1,0:T(8,128)S(1)} %get-tuple-element.19), custom_call_target="InvertDiagBlocksLowerTriangular" | custom-call | tf_op jit(solution)/shard_map/jit(_cho_solve)/triangular_solve | solution.py:71
  749.6 24.4 %all-gather.7.cloned.1.call-done = f32[16384,32]{0,1:T(8,128)} async-done(((f32[256,32]{0,1:T(8,128)}), f32[16384,32]{0,1:T(8,128)}) %all-gather.7.cloned.1.call-update) | async-done | bytes 2097168 | tf_op jit(solution)/shard_map/all_gather | solution.py:69
  774.0 2.2 copy.28
  776.2 0.2 bitcast_reduce_fusion
  776.4 0.2 fusion.54
  776.5 0.2 convolution_subtract_fusion.5
  776.8 0.2 fusion.56
  776.9 0.2 fusion.55
  777.1 0.2 convolution_subtract_fusion.4
  777.3 0.2 fusion.53
  777.6 6.3 convolution_subtract_fusion
  (50 shorter events, 0.9 us)
Async XLA Ops:
  7.2 537.0 %all-reduce.4.cloned.1.call-start = ((), (), s32[]{:S(2)}) async-start(), calls=%async_computation.2 | async-start | bytes 524288 | tf_op jit(solution)/shard_map/psum | solution.py:55
  10.3 4.9 slice-start
  12.4 2.8 slice-start.1
  23.7 3.8 copy-start
  27.4 627.0 %all-gather.5.cloned.1.call-start = ((), (), s32[]{:S(2)}) async-start(), calls=%async_computation | async-start | bytes 2129920 | tf_op jit(solution)/shard_map/all_gather | solution.py:69
  34.0 739.9 %all-gather.7.cloned.1.call-start = ((), (), s32[]{:S(2)}) async-start(), calls=%async_computation.1 | async-start | bytes 2129920 | tf_op jit(solution)/shard_map/all_gather | solution.py:69
  657.9 10.5 %copy-start.2 = (f32[1,64,512]{2,1,0:T(8,128)S(1)}, f32[1,64,512]{2,1,0:T(8,128)}, u32[]{:S(2)}) copy-start(f32[1,64,512]{2,1,0:T(8,128)} %get-tuple-element.38) | copy-start | bytes 393220
  777.6 6.3 copy-start.1
Sparse Core Ops, SparseCore 0:
  27.5 516.6 all-reduce.3
  546.6 107.6 all-gather.4
  668.6 105.3 all-gather.6
